TPU v7x, 128 devices: a whole 4x4x4 slice. The times are simulated.
128 devices in a mesh: section: 2 (over core), row: 32 (over z, y, x_hi), col: 2 (over x_lo).
Axes of the slice: x: 4 (x_hi: 2, x_lo: 2; x = x_hi * 2 + x_lo), y: 4, z: 4, core: 2. Of those that a mesh axis runs over, the one named last changes fastest.
Arguments:
- latents: bfloat16 [32, 4, 256, 1152], P('row', None, 'col'), may hold values from -6 to 6
- timesteps: int32 [32], P('row'), may hold values from 0 to 999
- lengths: int32 [32], P('row'), may hold values from 1 to 1024, 24576 in all
- patch_order: int32 [4], replicated, may hold values from 0 to 3, each once
- ada_weight: bfloat16 [2, 1152, 6, 1152], P('section', 'row', None, 'col'), may hold values from -0.1875 to 0.1875
- qkv_weight: bfloat16 [2, 1152, 3, 1152], P('section', 'row', None, 'col'), may hold values from -1 to 1
- out_weight: bfloat16 [2, 1152, 1152], P('section', 'col', 'row'), may hold values from -0.1875 to 0.1875
- up_weight: bfloat16 [2, 1152, 4608], P('section', 'row', 'col'), may hold values from -0.1875 to 0.1875
- down_weight: bfloat16 [2, 4608, 1152], P('section', 'col', 'row'), may hold values from -0.09375 to 0.09375
- stale_keys: bfloat16 [2, 32, 4, 256, 1152], P('section', 'row', None, None, 'col'), may hold values from -9 to 9
- stale_values: bfloat16 [2, 32, 4, 256, 1152], P('section', 'row', None, None, 'col'), may hold values from -6 to 6
Outputs:
- section_out: bfloat16 [2, 32, 4, 256, 1152], P('section', 'row', None, 'col')
Inputs may be any that keep to these rules, and one draw needn't show every extreme that they name: `lengths`: tokens that serve as keys in each request; some request has all 1024. `patch_order`: each of the 4 patches once.
All inputs are finite; a program needn't handle non-finite values. No bound on the sum of `lengths` on one device may be relied on, other than what follows from the above.
Results may differ from a plain program's by a relative error of at most 0.0095.
Values may be sent and summed in bfloat16 or wider, within the bound.
A program may use at most 128 MiB of HBM per device.

v0:
```python
import math
import jax
import jax.numpy as jnp
from jax import lax
from jax.sharding import PartitionSpec as P

D = 1152
HD = 72


def passed_along(shard, axis, by):
    size = lax.axis_size(axis)
    pairs = [(i, i + by) for i in range(size) if 0 <= i + by < size]
    return lax.ppermute(shard, axis, pairs)


def sinusoid(step_ids):
    half_width = D // 2
    frequency = jnp.exp(-math.log(10000.0) * jnp.arange(half_width, dtype=jnp.float32) / half_width)
    angles = step_ids.astype(jnp.float32)[:, None] * frequency[None, :]
    return jnp.concatenate([jnp.cos(angles), jnp.sin(angles)], axis=1)


def layer_norm(inputs):
    center = jnp.mean(inputs, axis=-1, keepdims=True)
    spread = jnp.mean(jnp.square(inputs - center), axis=-1, keepdims=True)
    return (inputs - center) * lax.rsqrt(spread + 1e-06)


def attend(queries, keys, values, valid_keys):
    scores = jnp.einsum(
        "bqhd,bkhd->bhqk", queries, keys, preferred_element_type=jnp.float32
    ) / math.sqrt(HD)
    scores = jnp.where(valid_keys[:, None, None, :], scores, -1e30)
    top_score = jnp.max(scores, axis=-1, keepdims=True)
    weights = jnp.exp(scores - top_score)
    totals = jnp.sum(weights, axis=-1)
    probs = weights.astype(jnp.bfloat16)
    mixed = jnp.einsum("bhqk,bkhd->bqhd", probs, values, preferred_element_type=jnp.float32)
    return (mixed / jnp.transpose(totals, (0, 2, 1))[..., None]).astype(jnp.bfloat16)


def put_slot(buffer, new_slot, patch_id, active):
    old_slot = lax.dynamic_index_in_dim(buffer, patch_id, 1, keepdims=False)
    return lax.dynamic_update_index_in_dim(
        buffer, jnp.where(active, new_slot, old_slot), patch_id, 1
    )


def local(
    latents,
    timesteps,
    lengths,
    patch_order,
    ada_weight,
    qkv_weight,
    out_weight,
    up_weight,
    down_weight,
    stale_keys,
    stale_values,
):
    section_id = lax.axis_index("section")
    ada_local = ada_weight[0]
    qkv_local = qkv_weight[0]
    up_local = up_weight[0]
    qkv_full, up_full, ada_full = (
        lax.all_gather(qkv_local, "row", axis=0, tiled=True),
        lax.all_gather(up_local, "row", axis=0, tiled=True),
        lax.all_gather(ada_local, "row", axis=0, tiled=True),
    )
    cond = jax.nn.silu(sinusoid(timesteps)).astype(jnp.bfloat16)
    mod_cols = jnp.einsum("rd,dkc->rkc", cond, ada_full, preferred_element_type=jnp.float32)
    out_full, down_full = (
        lax.all_gather(out_weight[0], "row", axis=1, tiled=True),
        lax.all_gather(down_weight[0], "row", axis=1, tiled=True),
    )
    modulation = lax.all_gather(mod_cols, "col", axis=2, tiled=True)
    shift_attn = modulation[:, 0][:, None, :]
    scale_attn = modulation[:, 1][:, None, :]
    gate_attn = modulation[:, 2][:, None, :]
    shift_mlp = modulation[:, 3][:, None, :]
    scale_mlp = modulation[:, 4][:, None, :]
    gate_mlp = modulation[:, 5][:, None, :]
    key_buffer = stale_keys[0]
    value_buffer = stale_values[0]
    req_local, patch_count, patch_tokens, head_cols = key_buffer.shape
    heads_local = head_cols // HD
    seq_len = patch_count * patch_tokens
    valid_keys = jnp.arange(seq_len, dtype=jnp.int32)[None, :] < lengths[:, None]
    local_tokens = latents.shape[2]
    width_full = latents.shape[3]
    results = jnp.zeros((req_local, patch_count, local_tokens, width_full), jnp.bfloat16)
    previous = jnp.zeros((req_local, local_tokens, width_full), jnp.bfloat16)
    for tick_index in range(patch_count + 1):
        position = tick_index - section_id
        active = (position >= 0) & (position < patch_count)
        patch_id = patch_order[jnp.clip(position, 0, patch_count - 1)]
        own_tokens = lax.dynamic_index_in_dim(latents, patch_id, 1, keepdims=False)
        if tick_index > 0:
            arrived = passed_along(previous, "section", 1)
            current = jnp.where(section_id == 0, own_tokens, arrived)
        else:
            current = own_tokens
        tokens_in = current.astype(jnp.float32)
        normed = (layer_norm(tokens_in) * (1.0 + scale_attn) + shift_attn).astype(jnp.bfloat16)
        whole = lax.all_gather(normed, "col", axis=1, tiled=True)
        projected = jnp.einsum(
            "rtd,dkc->rtkc", whole, qkv_full, preferred_element_type=jnp.float32
        ).astype(jnp.bfloat16)
        key_buffer = put_slot(key_buffer, projected[:, :, 1], patch_id, active)
        value_buffer = put_slot(value_buffer, projected[:, :, 2], patch_id, active)
        attended = attend(
            projected[:, :, 0].reshape(req_local, patch_tokens, heads_local, HD),
            key_buffer.reshape(req_local, seq_len, heads_local, HD),
            value_buffer.reshape(req_local, seq_len, heads_local, HD),
            valid_keys,
        ).reshape(req_local, patch_tokens, head_cols)
        attn_partial = jnp.einsum(
            "rtc,cd->rtd", attended, out_full, preferred_element_type=jnp.float32
        )
        attn_summed = lax.psum_scatter(
            attn_partial.astype(jnp.bfloat16), "col", scatter_dimension=1, tiled=True
        ).astype(jnp.float32)
        after_attn = tokens_in + gate_attn * attn_summed
        normed_mlp = (layer_norm(after_attn) * (1.0 + scale_mlp) + shift_mlp).astype(jnp.bfloat16)
        whole_mlp = lax.all_gather(normed_mlp, "col", axis=1, tiled=True)
        hidden = jax.nn.gelu(
            jnp.einsum("rtd,df->rtf", whole_mlp, up_full, preferred_element_type=jnp.float32),
            approximate=True,
        ).astype(jnp.bfloat16)
        mlp_partial = jnp.einsum(
            "rtf,fd->rtd", hidden, down_full, preferred_element_type=jnp.float32
        )
        mlp_summed = lax.psum_scatter(
            mlp_partial.astype(jnp.bfloat16), "col", scatter_dimension=1, tiled=True
        ).astype(jnp.float32)
        result = (after_attn + gate_mlp * mlp_summed).astype(jnp.bfloat16)
        results = put_slot(results, result, patch_id, active)
        previous = result
    return results[None]


def solution(mesh):
    return jax.shard_map(
        local,
        mesh=mesh,
        in_specs=(
            P("row", None, "col", None),
            P("row"),
            P("row"),
            P(),
            P("section", "row", None, "col"),
            P("section", "row", None, "col"),
            P("section", "col", "row"),
            P("section", "row", "col"),
            P("section", "col", "row"),
            P("section", "row", None, None, "col"),
            P("section", "row", None, None, "col"),
        ),
        out_specs=P("section", "row", None, "col", None),
        check_vma=False,
    )
```

profile of v0, /device:TPU:1, one launch (start us, length us, event | category | flops | bytes accessed | tf_op | source)
XLA Modules:
  0.0 1007.3 jit_solution(821713354570099396)
XLA Ops:
  22.2 64.5 %all-gather.17.cloned.1.call-done = bf16[1,576,1152]{1,0,2:T(2,128)(2,1)} async-done(((bf16[1,576,36]{1,0,2:T(2,128)(2,1)}), bf16[1,576,1152]{1,0,2:T(2,128)(2,1)}) %all-gather.17.cloned.1.call-update) | async-done | bytes 1327120 | tf_op jit(solution)/shard_map/all_gather | solution.py:75
  93.4 85.9 %all-gather.15.cloned.1.call-done = bf16[1,1152,3,576]{3,2,0,1:T(4,128)(2,1)} async-done(((bf16[1,36,3,576]{3,2,0,1:T(4,128)(2,1)}), bf16[1,1152,3,576]{3,2,0,1:T(4,128)(2,1)}) %all-gather.15.cloned.1.call-update) | async-done | bytes 3981328 | tf_op jit(solution)/shard_map/all_gather | solution.py:68
  179.3 11.3 %copy.44 = bf16[1,1152,3,576]{1,3,2,0:T(8,128)(2,1)} copy(bf16[1,1152,3,576]{3,2,0,1:T(4,128)(2,1)} %all-gather.15.cloned.1.call-done) | data formatting | bytes 7962624 | tf_op jit(solution)/shard_map/all_gather | solution.py:68
  190.6 115.0 %all-gather.13.cloned.1.call-done = bf16[1,1152,6,576]{3,2,0,1:T(8,128)(2,1)} async-done(((bf16[1,36,6,576]{3,2,0,1:T(8,128)(2,1)}), bf16[1,1152,6,576]{3,2,0,1:T(8,128)(2,1)}) %all-gather.13.cloned.1.call-update) | async-done | bytes 7962640 | tf_op jit(solution)/shard_map/all_gather | solution.py:70
  320.3 7.6 all_gather.50
  352.7 72.8 %all-gather.21.cloned.1.call-done = bf16[1,2304,1152]{1,0,2:T(2,128)(2,1)} async-done(((bf16[1,2304,36]{1,0,2:T(2,128)(2,1)}), bf16[1,2304,1152]{1,0,2:T(2,128)(2,1)}) %all-gather.21.cloned.1.call-update) | async-done | bytes 5308432 | tf_op jit(solution)/shard_map/all_gather | solution.py:76
  425.5 23.4 %copy.51 = bf16[1,2304,1152]{2,1,0:T(8,128)(2,1)} copy(bf16[1,2304,1152]{1,0,2:T(2,128)(2,1)} %all-gather.21.cloned.1.call-done) | data formatting | bytes 10616832 | tf_op jit(solution)/shard_map/all_gather | solution.py:76
  448.8 95.5 %all-gather.19.cloned.1.call-done = bf16[1,1152,2304]{2,0,1:T(2,128)(2,1)} async-done(((bf16[1,36,2304]{2,0,1:T(2,128)(2,1)}), bf16[1,1152,2304]{2,0,1:T(2,128)(2,1)}) %all-gather.19.cloned.1.call-update) | async-done | bytes 5308432 | tf_op jit(solution)/shard_map/all_gather | solution.py:69
  551.5 11.2 %reduce-scatter.11.cloned.1.call-done = bf16[1,128,1152]{2,1,0:T(8,128)(2,1)} async-done(((bf16[1,256,1152]{2,1,0:T(8,128)(2,1)}), bf16[1,128,1152]{2,1,0:T(8,128)(2,1)}) %reduce-scatter.11.cloned.1.call-update) | async-done | bytes 294928 | tf_op jit(solution)/shard_map/reduce_scatter | solution.py:122
  566.2 8.8 all_gather.53
  575.0 8.3 fusion.89
  583.4 19.8 %reduce-scatter.13.cloned.1.call-done = bf16[1,128,1152]{2,1,0:T(8,128)(2,1)} async-done(((bf16[1,256,1152]{2,1,0:T(8,128)(2,1)}), bf16[1,128,1152]{2,1,0:T(8,128)(2,1)}) %reduce-scatter.13.cloned.1.call-update) | async-done | bytes 294928 | tf_op jit(solution)/shard_map/reduce_scatter | solution.py:135
  612.4 8.4 all_gather.56
  643.8 19.9 %reduce-scatter.15.cloned.1.call-done = bf16[1,128,1152]{2,1,0:T(8,128)(2,1)} async-done(((bf16[1,256,1152]{2,1,0:T(8,128)(2,1)}), bf16[1,128,1152]{2,1,0:T(8,128)(2,1)}) %reduce-scatter.15.cloned.1.call-update) | async-done | bytes 294928 | tf_op jit(solution)/shard_map/reduce_scatter | solution.py:122
  667.2 9.0 all_gather.57
  676.1 8.2 fusion.86
  685.4 18.7 %reduce-scatter.17.cloned.1.call-done = bf16[1,128,1152]{2,1,0:T(8,128)(2,1)} async-done(((bf16[1,256,1152]{2,1,0:T(8,128)(2,1)}), bf16[1,128,1152]{2,1,0:T(8,128)(2,1)}) %reduce-scatter.17.cloned.1.call-update) | async-done | bytes 294928 | tf_op jit(solution)/shard_map/reduce_scatter | solution.py:135
  711.4 8.7 all_gather.58
  743.0 19.7 %reduce-scatter.19.cloned.1.call-done = bf16[1,128,1152]{2,1,0:T(8,128)(2,1)} async-done(((bf16[1,256,1152]{2,1,0:T(8,128)(2,1)}), bf16[1,128,1152]{2,1,0:T(8,128)(2,1)}) %reduce-scatter.19.cloned.1.call-update) | async-done | bytes 294928 | tf_op jit(solution)/shard_map/reduce_scatter | solution.py:122
  766.2 8.7 all_gather.59
  774.9 8.2 fusion.83
  784.2 18.7 %reduce-scatter.21.cloned.1.call-done = bf16[1,128,1152]{2,1,0:T(8,128)(2,1)} async-done(((bf16[1,256,1152]{2,1,0:T(8,128)(2,1)}), bf16[1,128,1152]{2,1,0:T(8,128)(2,1)}) %reduce-scatter.21.cloned.1.call-update) | async-done | bytes 294928 | tf_op jit(solution)/shard_map/reduce_scatter | solution.py:135
  810.2 8.6 all_gather.60
  841.7 19.7 %reduce-scatter.23.cloned.1.call-done = bf16[1,128,1152]{2,1,0:T(8,128)(2,1)} async-done(((bf16[1,256,1152]{2,1,0:T(8,128)(2,1)}), bf16[1,128,1152]{2,1,0:T(8,128)(2,1)}) %reduce-scatter.23.cloned.1.call-update) | async-done | bytes 294928 | tf_op jit(solution)/shard_map/reduce_scatter | solution.py:122
  865.0 8.8 all_gather.61
  873.7 8.2 fusion.80
  883.0 18.8 %reduce-scatter.25.cloned.1.call-done = bf16[1,128,1152]{2,1,0:T(8,128)(2,1)} async-done(((bf16[1,256,1152]{2,1,0:T(8,128)(2,1)}), bf16[1,128,1152]{2,1,0:T(8,128)(2,1)}) %reduce-scatter.25.cloned.1.call-update) | async-done | bytes 294928 | tf_op jit(solution)/shard_map/reduce_scatter | solution.py:135
  909.1 8.4 all_gather.62
  938.4 19.9 %reduce-scatter.27.cloned.1.call-done = bf16[1,128,1152]{2,1,0:T(8,128)(2,1)} async-done(((bf16[1,256,1152]{2,1,0:T(8,128)(2,1)}), bf16[1,128,1152]{2,1,0:T(8,128)(2,1)}) %reduce-scatter.27.cloned.1.call-update) | async-done | bytes 294928 | tf_op jit(solution)/shard_map/reduce_scatter | solution.py:122
  961.8 8.8 all_gather.63
  970.6 8.2 fusion.77
  981.2 17.3 %reduce-scatter.29.cloned.1.call-done = bf16[1,128,1152]{2,1,0:T(8,128)(2,1)} async-done(((bf16[1,256,1152]{2,1,0:T(8,128)(2,1)}), bf16[1,128,1152]{2,1,0:T(8,128)(2,1)}) %reduce-scatter.29.cloned.1.call-update) | async-done | bytes 294928 | tf_op jit(solution)/shard_map/reduce_scatter | solution.py:135
  (265 shorter events, 203.3 us)
Async XLA Ops:
  6.5 80.2 %all-gather.17.cloned.1.call-start = ((), (), s32[]{:S(2)}) async-start(), calls=%async_computation.22 | async-start | bytes 3041280 | tf_op jit(solution)/shard_map/all_gather | solution.py:75
  8.2 171.1 %all-gather.15.cloned.1.call-start = ((), (), s32[]{:S(2)}) async-start(), calls=%async_computation.21 | async-start | bytes 6082560 | tf_op jit(solution)/shard_map/all_gather | solution.py:68
  9.9 295.8 %all-gather.13.cloned.1.call-start = ((), (), s32[]{:S(2)}) async-start(), calls=%async_computation.20 | async-start | bytes 12165120 | tf_op jit(solution)/shard_map/all_gather | solution.py:70
  11.7 413.8 %all-gather.21.cloned.1.call-start = ((), (), s32[]{:S(2)}) async-start(), calls=%async_computation.24 | async-start | bytes 10948608 | tf_op jit(solution)/shard_map/all_gather | solution.py:76
  13.7 530.6 %all-gather.19.cloned.1.call-start = ((), (), s32[]{:S(2)}) async-start(), calls=%async_computation.23 | async-start | bytes 10948608 | tf_op jit(solution)/shard_map/all_gather | solution.py:69
  14.8 547.9 %reduce-scatter.11.cloned.1.call-start = ((), (), s32[]{:S(2)}) async-start(), calls=%async_computation.10 | async-start | bytes 884736 | tf_op jit(solution)/shard_map/reduce_scatter | solution.py:122
  352.6 250.6 %reduce-scatter.13.cloned.1.call-start = ((), (), s32[]{:S(2)}) async-start(), calls=%async_computation.11 | async-start | bytes 884736 | tf_op jit(solution)/shard_map/reduce_scatter | solution.py:135
  583.4 80.3 %reduce-scatter.15.cloned.1.call-start = ((), (), s32[]{:S(2)}) async-start(), calls=%async_computation.12 | async-start | bytes 884736 | tf_op jit(solution)/shard_map/reduce_scatter | solution.py:122
  606.4 3.7 collective-permute-start
  642.2 23.8 %copy-start.20 = (f32[1152]{0:T(1024)S(1)}, f32[1152]{0:T(1024)}, u32[]{:S(2)}) copy-start(f32[1152]{0:T(1024)} %get-tuple-element.6) | copy-start | bytes 13828
  642.2 23.8 %copy-start.24 = (f32[1152]{0:T(1024)S(1)}, f32[1152]{0:T(1024)}, u32[]{:S(2)}) copy-start(f32[1152]{0:T(1024)} %get-tuple-element.7) | copy-start | bytes 13828
  643.7 60.4 %reduce-scatter.17.cloned.1.call-start = ((), (), s32[]{:S(2)}) async-start(), calls=%async_computation.13 | async-start | bytes 884736 | tf_op jit(solution)/shard_map/reduce_scatter | solution.py:135
  676.1 28.0 %copy-start.2 = (bf16[1,128,1152]{2,1,0:T(8,128)(2,1)S(1)}, bf16[1,128,1152]{2,1,0:T(8,128)(2,1)}, u32[]{:S(2)}) copy-start(bf16[1,128,1152]{2,1,0:T(8,128)(2,1)} %reduce-scatter.15.cloned.1.call-done) | copy-start | bytes 884740
  684.3 26.8 %copy-start.29 = (f32[1152]{0:T(1024)S(1)}, f32[1152]{0:T(1024)}, u32[]{:S(2)}) copy-start(f32[1152]{0:T(1024)} %copy-done.28) | copy-start | bytes 13828
  684.3 26.8 %copy-start.33 = (f32[1152]{0:T(1024)S(1)}, f32[1152]{0:T(1024)}, u32[]{:S(2)}) copy-start(f32[1152]{0:T(1024)} %copy-done.32) | copy-start | bytes 13828
  684.4 78.3 %reduce-scatter.19.cloned.1.call-start = ((), (), s32[]{:S(2)}) async-start(), calls=%async_computation.14 | async-start | bytes 884736 | tf_op jit(solution)/shard_map/reduce_scatter | solution.py:122
  706.1 3.7 collective-permute-start.1
  743.0 59.9 %reduce-scatter.21.cloned.1.call-start = ((), (), s32[]{:S(2)}) async-start(), calls=%async_computation.15 | async-start | bytes 884736 | tf_op jit(solution)/shard_map/reduce_scatter | solution.py:135
  774.9 28.0 %copy-start.3 = (bf16[1,128,1152]{2,1,0:T(8,128)(2,1)S(1)}, bf16[1,128,1152]{2,1,0:T(8,128)(2,1)}, u32[]{:S(2)}) copy-start(bf16[1,128,1152]{2,1,0:T(8,128)(2,1)} %reduce-scatter.19.cloned.1.call-done) | copy-start | bytes 884740
  783.1 26.8 %copy-start.30 = (f32[1152]{0:T(1024)S(1)}, f32[1152]{0:T(1024)}, u32[]{:S(2)}) copy-start(f32[1152]{0:T(1024)} %copy-done.28) | copy-start | bytes 13828
  783.1 26.8 %copy-start.34 = (f32[1152]{0:T(1024)S(1)}, f32[1152]{0:T(1024)}, u32[]{:S(2)}) copy-start(f32[1152]{0:T(1024)} %copy-done.32) | copy-start | bytes 13828
  783.2 78.3 %reduce-scatter.23.cloned.1.call-start = ((), (), s32[]{:S(2)}) async-start(), calls=%async_computation.16 | async-start | bytes 884736 | tf_op jit(solution)/shard_map/reduce_scatter | solution.py:122
  804.9 3.7 collective-permute-start.2
  841.7 60.1 %reduce-scatter.25.cloned.1.call-start = ((), (), s32[]{:S(2)}) async-start(), calls=%async_computation.17 | async-start | bytes 884736 | tf_op jit(solution)/shard_map/reduce_scatter | solution.py:135
  873.7 28.1 %copy-start.4 = (bf16[1,128,1152]{2,1,0:T(8,128)(2,1)S(1)}, bf16[1,128,1152]{2,1,0:T(8,128)(2,1)}, u32[]{:S(2)}) copy-start(bf16[1,128,1152]{2,1,0:T(8,128)(2,1)} %reduce-scatter.23.cloned.1.call-done) | copy-start | bytes 884740
  881.9 26.9 %copy-start.31 = (f32[1152]{0:T(1024)S(1)}, f32[1152]{0:T(1024)}, u32[]{:S(2)}) copy-start(f32[1152]{0:T(1024)} %copy-done.28) | copy-start | bytes 13828
  881.9 26.9 %copy-start.35 = (f32[1152]{0:T(1024)S(1)}, f32[1152]{0:T(1024)}, u32[]{:S(2)}) copy-start(f32[1152]{0:T(1024)} %copy-done.32) | copy-start | bytes 13828
  882.0 76.3 %reduce-scatter.27.cloned.1.call-start = ((), (), s32[]{:S(2)}) async-start(), calls=%async_computation.18 | async-start | bytes 884736 | tf_op jit(solution)/shard_map/reduce_scatter | solution.py:122
  903.8 3.7 collective-permute-start.3
  936.8 23.8 %copy-start.23 = (f32[1152]{0:T(1024)S(1)}, f32[1152]{0:T(1024)}, u32[]{:S(2)}) copy-start(f32[1152]{0:T(1024)} %get-tuple-element.6) | copy-start | bytes 13828
  936.8 23.8 %copy-start.27 = (f32[1152]{0:T(1024)S(1)}, f32[1152]{0:T(1024)}, u32[]{:S(2)}) copy-start(f32[1152]{0:T(1024)} %get-tuple-element.7) | copy-start | bytes 13828
  938.4 60.2 %reduce-scatter.29.cloned.1.call-start = ((), (), s32[]{:S(2)}) async-start(), calls=%async_computation.19 | async-start | bytes 884736 | tf_op jit(solution)/shard_map/reduce_scatter | solution.py:135
  (35 other events, 221.2 us)
Sparse Core Ops, SparseCore 0:
  10.5 76.1 all-gather.16
  89.7 89.5 all-gather.14
  182.3 123.2 all-gather.12
  308.5 116.9 all-gather.20
  428.4 115.8 all-gather.18
  546.5 16.1 reduce-scatter.10
  583.5 19.6 reduce-scatter.12
  643.8 19.7 reduce-scatter.14
  684.5 19.5 reduce-scatter.16
  743.1 19.5 reduce-scatter.18
  783.3 19.5 reduce-scatter.20
  841.8 19.5 reduce-scatter.22
  882.1 19.6 reduce-scatter.24
  938.5 19.7 reduce-scatter.26
  978.9 19.5 reduce-scatter.28
where the time goes:
time: 1010 us
  waiting for transfers between devices  619 us (61%)
  local copies, waits for them, and re-layouts  121 us (12%)
  matrix products  96.2 us (10%)
  blocking collectives  89 us (9%)
  other arithmetic  51 us (5%)
  between operations  25.1 us (2%)
    all_gather x1, waiting for transfers between devices, local(): lax.all_gather(ada_local, 'row', axis=0, tiled=True)  115 us
    all_gather x1, waiting for transfers between devices, local(): lax.all_gather(up_local, 'row', axis=0, tiled=True)  95.5 us
    reduce_scatter x5, waiting for transfers between devices, local(): lax.psum_scatter(mlp_partial.astype(jnp.bfloat16), 'col', scatter_dimensi...  93.3 us
    reduce_scatter x5, waiting for transfers between devices, local(): lax.psum_scatter(attn_partial.astype(jnp.bfloat16), 'col', scatter_dimens...  90.3 us
    all_gather x1, waiting for transfers between devices, local(): lax.all_gather(qkv_local, 'row', axis=0, tiled=True)  85.9 us
    all_gather x1, waiting for transfers between devices, local(): lax.all_gather(down_weight[0], 'row', axis=1, tiled=True)  72.8 us
    all_gather x1, waiting for transfers between devices, local(): lax.all_gather(out_weight[0], 'row', axis=1, tiled=True)  64.5 us
    all_gather x5, blocking collectives, local(): whole_mlp = lax.all_gather(normed_mlp, 'col', axis=1, tiled=True)  44.1 us
  transfers between devices with their start and end apart: 19, of which 19 were waited for; matrix products, arithmetic and copies ran while one was open for 10% of the time, Pallas kernels for 0%

commit v1 on v0

--- a/solution.py
+++ b/solution.py
@@ -124,7 +124,9 @@
         ).astype(jnp.float32)
         after_attn = tokens_in + gate_attn * attn_summed
         normed_mlp = (layer_norm(after_attn) * (1.0 + scale_mlp) + shift_mlp).astype(jnp.bfloat16)
-        whole_mlp = lax.all_gather(normed_mlp, "col", axis=1, tiled=True)
+        whole_mlp = jnp.concatenate(
+            lax.all_to_all(jnp.stack([normed_mlp] * lax.axis_size("col")), "col", 0, 0), axis=1
+        )
         hidden = jax.nn.gelu(
             jnp.einsum("rtd,df->rtf", whole_mlp, up_full, preferred_element_type=jnp.float32),
             approximate=True,

time: 1010 us -> 1070 us (1.059)
  waiting for transfers between devices: 619 us -> 663 us
    all_to_all x0 -> x4, blocking collectives: none -> 45.2 us  [local(): lax.all_to_all(jnp.stack([normed_mlp] * lax.axis_size('col')), 'col', 0, 0)]
    all_gather x5 -> x0, blocking collectives: 44.1 us -> none  [local(): whole_mlp = lax.all_gather(normed_mlp, 'col', axis=1, tiled=True)]
    all_gather x1, waiting for transfers between devices: 72.8 us -> 113 us  [local(): lax.all_gather(down_weight[0], 'row', axis=1, tiled=True)]
  transfers between devices with their start and end apart: 19 -> 20, of which waited for: 19 -> 19; matrix products, arithmetic and copies ran while one was open for 10% -> 7% of each run, Pallas kernels for 0% -> 0%
where the time goes in v1:
time: 1070 us; the launch traced here: 1060 us
  waiting for transfers between devices  663 us (62%)
  local copies, waits for them, and re-layouts  122 us (11%)
  matrix products  96.7 us (9%)
  blocking collectives  90.3 us (8%)
  other arithmetic  52.2 us (5%)
  between operations  25 us (2%)
    all_gather x1, waiting for transfers between devices, local(): lax.all_gather(ada_local, 'row', axis=0, tiled=True)  115 us
    all_gather x1, waiting for transfers between devices, local(): lax.all_gather(down_weight[0], 'row', axis=1, tiled=True)  113 us
    all_gather x1, waiting for transfers between devices, local(): lax.all_gather(up_local, 'row', axis=0, tiled=True)  95.9 us
    reduce_scatter x5, waiting for transfers between devices, local(): lax.psum_scatter(attn_partial.astype(jnp.bfloat16), 'col', scatter_dimens...  93.2 us
    reduce_scatter x5, waiting for transfers between devices, local(): lax.psum_scatter(mlp_partial.astype(jnp.bfloat16), 'col', scatter_dimensi...  89.8 us
    all_gather x1, waiting for transfers between devices, local(): lax.all_gather(qkv_local, 'row', axis=0, tiled=True)  86 us
    all_gather x1, waiting for transfers between devices, local(): lax.all_gather(out_weight[0], 'row', axis=1, tiled=True)  67.6 us
    all_to_all x4, blocking collectives, local(): lax.all_to_all(jnp.stack([normed_mlp] * lax.axis_size('col')), 'col', 0, 0)  45.2 us
  transfers between devices with their start and end apart: 20, of which 19 were waited for; matrix products, arithmetic and copies ran while one was open for 7% of the time, Pallas kernels for 0%

profile of v1, /device:TPU:1, one launch (start us, length us, event | category | flops | bytes accessed | tf_op | source)
XLA Modules:
  0.0 1058.8 jit_solution(2936013871510459259)
XLA Ops:
  19.1 67.6 %all-gather.17.cloned.1.call-done = bf16[1,576,1152]{1,0,2:T(2,128)(2,1)} async-done(((bf16[1,576,36]{1,0,2:T(2,128)(2,1)}), bf16[1,576,1152]{1,0,2:T(2,128)(2,1)}) %all-gather.17.cloned.1.call-update) | async-done | bytes 1327120 | tf_op jit(solution)/shard_map/all_gather | solution.py:75
  93.3 86.0 %all-gather.15.cloned.1.call-done = bf16[1,1152,3,576]{3,2,0,1:T(4,128)(2,1)} async-done(((bf16[1,36,3,576]{3,2,0,1:T(4,128)(2,1)}), bf16[1,1152,3,576]{3,2,0,1:T(4,128)(2,1)}) %all-gather.15.cloned.1.call-update) | async-done | bytes 3981328 | tf_op jit(solution)/shard_map/all_gather | solution.py:68
  179.3 11.3 %copy.44 = bf16[1,1152,3,576]{1,3,2,0:T(8,128)(2,1)} copy(bf16[1,1152,3,576]{3,2,0,1:T(4,128)(2,1)} %all-gather.15.cloned.1.call-done) | data formatting | bytes 7962624 | tf_op jit(solution)/shard_map/all_gather | solution.py:68
  190.6 115.0 %all-gather.13.cloned.1.call-done = bf16[1,1152,6,576]{3,2,0,1:T(8,128)(2,1)} async-done(((bf16[1,36,6,576]{3,2,0,1:T(8,128)(2,1)}), bf16[1,1152,6,576]{3,2,0,1:T(8,128)(2,1)}) %all-gather.13.cloned.1.call-update) | async-done | bytes 7962640 | tf_op jit(solution)/shard_map/all_gather | solution.py:70
  320.3 7.5 all_gather.35
  356.5 14.4 %reduce-scatter.11.cloned.1.call-done = bf16[1,128,1152]{2,1,0:T(8,128)(2,1)} async-done(((bf16[1,256,1152]{2,1,0:T(8,128)(2,1)}), bf16[1,128,1152]{2,1,0:T(8,128)(2,1)}) %reduce-scatter.11.cloned.1.call-update) | async-done | bytes 294928 | tf_op jit(solution)/shard_map/reduce_scatter | solution.py:122
  379.8 113.1 %all-gather.21.cloned.1.call-done = bf16[1,2304,1152]{1,0,2:T(2,128)(2,1)} async-done(((bf16[1,2304,36]{1,0,2:T(2,128)(2,1)}), bf16[1,2304,1152]{1,0,2:T(2,128)(2,1)}) %all-gather.21.cloned.1.call-update) | async-done | bytes 5308432 | tf_op jit(solution)/shard_map/all_gather | solution.py:76
  492.8 23.4 %copy.51 = bf16[1,2304,1152]{2,1,0:T(8,128)(2,1)} copy(bf16[1,2304,1152]{1,0,2:T(2,128)(2,1)} %all-gather.21.cloned.1.call-done) | data formatting | bytes 10616832 | tf_op jit(solution)/shard_map/all_gather | solution.py:76
  516.2 95.9 %all-gather.19.cloned.1.call-done = bf16[1,1152,2304]{2,0,1:T(2,128)(2,1)} async-done(((bf16[1,36,2304]{2,0,1:T(2,128)(2,1)}), bf16[1,1152,2304]{2,0,1:T(2,128)(2,1)}) %all-gather.19.cloned.1.call-update) | async-done | bytes 5308432 | tf_op jit(solution)/shard_map/all_gather | solution.py:69
  612.1 7.2 copy.62
  619.4 8.3 fusion.89
  627.8 16.2 %reduce-scatter.13.cloned.1.call-done = bf16[1,128,1152]{2,1,0:T(8,128)(2,1)} async-done(((bf16[1,256,1152]{2,1,0:T(8,128)(2,1)}), bf16[1,128,1152]{2,1,0:T(8,128)(2,1)}) %reduce-scatter.13.cloned.1.call-update) | async-done | bytes 294928 | tf_op jit(solution)/shard_map/reduce_scatter | solution.py:137
  653.2 8.8 all_gather.40
  684.9 19.5 %reduce-scatter.15.cloned.1.call-done = bf16[1,128,1152]{2,1,0:T(8,128)(2,1)} async-done(((bf16[1,256,1152]{2,1,0:T(8,128)(2,1)}), bf16[1,128,1152]{2,1,0:T(8,128)(2,1)}) %reduce-scatter.15.cloned.1.call-update) | async-done | bytes 294928 | tf_op jit(solution)/shard_map/reduce_scatter | solution.py:122
  708.0 11.6 %all_to_all.25 = bf16[2,1,128,1152]{3,2,1,0:T(8,128)(2,1)} all-to-all(bf16[2,1,128,1152]{3,2,1,0:T(8,128)(2,1)S(1)} %pad_maximum_fusion.1), channel_id=1, replica_groups=mesh['section'=2,'row'=32,'col'=2] {'col'}, dimensions={0} | all-to-all | bytes 1179648 | tf_op jit(solution)/shard_map/all_to_all | solution.py:128
  719.6 8.4 fusion.86
  729.1 18.7 %reduce-scatter.17.cloned.1.call-done = bf16[1,128,1152]{2,1,0:T(8,128)(2,1)} async-done(((bf16[1,256,1152]{2,1,0:T(8,128)(2,1)}), bf16[1,128,1152]{2,1,0:T(8,128)(2,1)}) %reduce-scatter.17.cloned.1.call-update) | async-done | bytes 294928 | tf_op jit(solution)/shard_map/reduce_scatter | solution.py:137
  755.1 8.6 all_gather.41
  786.6 19.7 %reduce-scatter.19.cloned.1.call-done = bf16[1,128,1152]{2,1,0:T(8,128)(2,1)} async-done(((bf16[1,256,1152]{2,1,0:T(8,128)(2,1)}), bf16[1,128,1152]{2,1,0:T(8,128)(2,1)}) %reduce-scatter.19.cloned.1.call-update) | async-done | bytes 294928 | tf_op jit(solution)/shard_map/reduce_scatter | solution.py:122
  809.9 11.4 %all_to_all.26 = bf16[2,1,128,1152]{3,2,1,0:T(8,128)(2,1)} all-to-all(bf16[2,1,128,1152]{3,2,1,0:T(8,128)(2,1)S(1)} %pad_maximum_fusion.2), channel_id=1, replica_groups=mesh['section'=2,'row'=32,'col'=2] {'col'}, dimensions={0} | all-to-all | bytes 1179648 | tf_op jit(solution)/shard_map/all_to_all | solution.py:128
  821.3 8.4 fusion.83
  830.8 18.7 %reduce-scatter.21.cloned.1.call-done = bf16[1,128,1152]{2,1,0:T(8,128)(2,1)} async-done(((bf16[1,256,1152]{2,1,0:T(8,128)(2,1)}), bf16[1,128,1152]{2,1,0:T(8,128)(2,1)}) %reduce-scatter.21.cloned.1.call-update) | async-done | bytes 294928 | tf_op jit(solution)/shard_map/reduce_scatter | solution.py:137
  856.8 8.4 all_gather.42
  888.2 19.9 %reduce-scatter.23.cloned.1.call-done = bf16[1,128,1152]{2,1,0:T(8,128)(2,1)} async-done(((bf16[1,256,1152]{2,1,0:T(8,128)(2,1)}), bf16[1,128,1152]{2,1,0:T(8,128)(2,1)}) %reduce-scatter.23.cloned.1.call-update) | async-done | bytes 294928 | tf_op jit(solution)/shard_map/reduce_scatter | solution.py:122
  911.6 11.4 %all_to_all.27 = bf16[2,1,128,1152]{3,2,1,0:T(8,128)(2,1)} all-to-all(bf16[2,1,128,1152]{3,2,1,0:T(8,128)(2,1)S(1)} %pad_maximum_fusion.3), channel_id=1, replica_groups=mesh['section'=2,'row'=32,'col'=2] {'col'}, dimensions={0} | all-to-all | bytes 1179648 | tf_op jit(solution)/shard_map/all_to_all | solution.py:128
  923.0 8.4 fusion.80
  932.5 18.7 %reduce-scatter.25.cloned.1.call-done = bf16[1,128,1152]{2,1,0:T(8,128)(2,1)} async-done(((bf16[1,256,1152]{2,1,0:T(8,128)(2,1)}), bf16[1,128,1152]{2,1,0:T(8,128)(2,1)}) %reduce-scatter.25.cloned.1.call-update) | async-done | bytes 294928 | tf_op jit(solution)/shard_map/reduce_scatter | solution.py:137
  958.5 8.6 all_gather.43
  988.0 19.7 %reduce-scatter.27.cloned.1.call-done = bf16[1,128,1152]{2,1,0:T(8,128)(2,1)} async-done(((bf16[1,256,1152]{2,1,0:T(8,128)(2,1)}), bf16[1,128,1152]{2,1,0:T(8,128)(2,1)}) %reduce-scatter.27.cloned.1.call-update) | async-done | bytes 294928 | tf_op jit(solution)/shard_map/reduce_scatter | solution.py:122
  1011.3 10.7 %all_to_all.28 = bf16[2,1,128,1152]{3,2,1,0:T(8,128)(2,1)S(1)} all-to-all(bf16[2,1,128,1152]{3,2,1,0:T(8,128)(2,1)S(1)} %pad_maximum_fusion.4), channel_id=1, replica_groups=mesh['section'=2,'row'=32,'col'=2] {'col'}, dimensions={0} | all-to-all | bytes 1179648 | tf_op jit(solution)/shard_map/all_to_all | solution.py:128
  1022.1 8.2 fusion.77
  1032.7 17.4 %reduce-scatter.29.cloned.1.call-done = bf16[1,128,1152]{2,1,0:T(8,128)(2,1)} async-done(((bf16[1,256,1152]{2,1,0:T(8,128)(2,1)}), bf16[1,128,1152]{2,1,0:T(8,128)(2,1)}) %reduce-scatter.29.cloned.1.call-update) | async-done | bytes 294928 | tf_op jit(solution)/shard_map/reduce_scatter | solution.py:137
  (269 shorter events, 202.6 us)
Async XLA Ops:
  6.5 80.2 %all-gather.17.cloned.1.call-start = ((), (), s32[]{:S(2)}) async-start(), calls=%async_computation.27 | async-start | bytes 3041280 | tf_op jit(solution)/shard_map/all_gather | solution.py:75
  8.2 171.1 %all-gather.15.cloned.1.call-start = ((), (), s32[]{:S(2)}) async-start(), calls=%async_computation.26 | async-start | bytes 6082560 | tf_op jit(solution)/shard_map/all_gather | solution.py:68
  9.9 295.8 %all-gather.13.cloned.1.call-start = ((), (), s32[]{:S(2)}) async-start(), calls=%async_computation.25 | async-start | bytes 12165120 | tf_op jit(solution)/shard_map/all_gather | solution.py:70
  11.7 359.2 %reduce-scatter.11.cloned.1.call-start = ((), (), s32[]{:S(2)}) async-start(), calls=%async_computation.15 | async-start | bytes 884736 | tf_op jit(solution)/shard_map/reduce_scatter | solution.py:122
  352.6 140.3 %all-gather.21.cloned.1.call-start = ((), (), s32[]{:S(2)}) async-start(), calls=%async_computation.29 | async-start | bytes 10948608 | tf_op jit(solution)/shard_map/all_gather | solution.py:76
  354.5 257.6 %all-gather.19.cloned.1.call-start = ((), (), s32[]{:S(2)}) async-start(), calls=%async_computation.28 | async-start | bytes 10948608 | tf_op jit(solution)/shard_map/all_gather | solution.py:69
  375.3 244.1 %all-to-all-start = ((bf16[2,1,128,1152]{3,2,1,0:T(8,128)(2,1)}), bf16[2,1,128,1152]{3,2,1,0:T(8,128)(2,1)}, u32[]{:S(2)}, u32[]{:S(2)}) async-start(bf16[2,1,128,1152]{3,2,1,0:T(8,128)(2,1)} %pad_maximum_fusion), calls=%async_computation.1 | async-start | bytes 1179648 | tf_op jit(solution)/shard_map/all_to_all | solution.py:128
  379.5 264.5 %reduce-scatter.13.cloned.1.call-start = ((), (), s32[]{:S(2)}) async-start(), calls=%async_computation.16 | async-start | bytes 884736 | tf_op jit(solution)/shard_map/reduce_scatter | solution.py:137
  627.7 76.7 %reduce-scatter.15.cloned.1.call-start = ((), (), s32[]{:S(2)}) async-start(), calls=%async_computation.17 | async-start | bytes 884736 | tf_op jit(solution)/shard_map/reduce_scatter | solution.py:122
  647.1 3.7 collective-permute-start
  684.9 62.9 %reduce-scatter.17.cloned.1.call-start = ((), (), s32[]{:S(2)}) async-start(), calls=%async_computation.18 | async-start | bytes 884736 | tf_op jit(solution)/shard_map/reduce_scatter | solution.py:137
  719.6 28.2 %copy-start.2 = (bf16[1,128,1152]{2,1,0:T(8,128)(2,1)S(1)}, bf16[1,128,1152]{2,1,0:T(8,128)(2,1)}, u32[]{:S(2)}) copy-start(bf16[1,128,1152]{2,1,0:T(8,128)(2,1)} %reduce-scatter.15.cloned.1.call-done) | copy-start | bytes 884740
  728.0 26.8 %copy-start.30 = (f32[1152]{0:T(1024)S(1)}, f32[1152]{0:T(1024)}, u32[]{:S(2)}) copy-start(f32[1152]{0:T(1024)} %copy-done.29) | copy-start | bytes 13828
  728.0 26.8 %copy-start.34 = (f32[1152]{0:T(1024)S(1)}, f32[1152]{0:T(1024)}, u32[]{:S(2)}) copy-start(f32[1152]{0:T(1024)} %copy-done.33) | copy-start | bytes 13828
  728.0 78.3 %reduce-scatter.19.cloned.1.call-start = ((), (), s32[]{:S(2)}) async-start(), calls=%async_computation.19 | async-start | bytes 884736 | tf_op jit(solution)/shard_map/reduce_scatter | solution.py:122
  749.8 3.7 collective-permute-start.1
  786.6 62.9 %reduce-scatter.21.cloned.1.call-start = ((), (), s32[]{:S(2)}) async-start(), calls=%async_computation.20 | async-start | bytes 884736 | tf_op jit(solution)/shard_map/reduce_scatter | solution.py:137
  821.3 28.2 %copy-start.3 = (bf16[1,128,1152]{2,1,0:T(8,128)(2,1)S(1)}, bf16[1,128,1152]{2,1,0:T(8,128)(2,1)}, u32[]{:S(2)}) copy-start(bf16[1,128,1152]{2,1,0:T(8,128)(2,1)} %reduce-scatter.19.cloned.1.call-done) | copy-start | bytes 884740
  829.7 26.8 %copy-start.31 = (f32[1152]{0:T(1024)S(1)}, f32[1152]{0:T(1024)}, u32[]{:S(2)}) copy-start(f32[1152]{0:T(1024)} %copy-done.29) | copy-start | bytes 13828
  829.7 26.8 %copy-start.35 = (f32[1152]{0:T(1024)S(1)}, f32[1152]{0:T(1024)}, u32[]{:S(2)}) copy-start(f32[1152]{0:T(1024)} %copy-done.33) | copy-start | bytes 13828
  829.7 78.3 %reduce-scatter.23.cloned.1.call-start = ((), (), s32[]{:S(2)}) async-start(), calls=%async_computation.21 | async-start | bytes 884736 | tf_op jit(solution)/shard_map/reduce_scatter | solution.py:122
  851.5 3.7 collective-permute-start.2
  886.5 23.8 %copy-start.23 = (f32[1152]{0:T(1024)S(1)}, f32[1152]{0:T(1024)}, u32[]{:S(2)}) copy-start(f32[1152]{0:T(1024)} %get-tuple-element.6) | copy-start | bytes 13828
  886.6 23.8 %copy-start.27 = (f32[1152]{0:T(1024)S(1)}, f32[1152]{0:T(1024)}, u32[]{:S(2)}) copy-start(f32[1152]{0:T(1024)} %get-tuple-element.7) | copy-start | bytes 13828
  888.1 63.1 %reduce-scatter.25.cloned.1.call-start = ((), (), s32[]{:S(2)}) async-start(), calls=%async_computation.22 | async-start | bytes 884736 | tf_op jit(solution)/shard_map/reduce_scatter | solution.py:137
  923.0 28.2 %copy-start.4 = (bf16[1,128,1152]{2,1,0:T(8,128)(2,1)S(1)}, bf16[1,128,1152]{2,1,0:T(8,128)(2,1)}, u32[]{:S(2)}) copy-start(bf16[1,128,1152]{2,1,0:T(8,128)(2,1)} %reduce-scatter.23.cloned.1.call-done) | copy-start | bytes 884740
  931.4 26.8 %copy-start.32 = (f32[1152]{0:T(1024)S(1)}, f32[1152]{0:T(1024)}, u32[]{:S(2)}) copy-start(f32[1152]{0:T(1024)} %copy-done.29) | copy-start | bytes 13828
  931.4 26.8 %copy-start.36 = (f32[1152]{0:T(1024)S(1)}, f32[1152]{0:T(1024)}, u32[]{:S(2)}) copy-start(f32[1152]{0:T(1024)} %copy-done.33) | copy-start | bytes 13828
  931.4 76.3 %reduce-scatter.27.cloned.1.call-start = ((), (), s32[]{:S(2)}) async-start(), calls=%async_computation.23 | async-start | bytes 884736 | tf_op jit(solution)/shard_map/reduce_scatter | solution.py:122
  953.2 3.7 collective-permute-start.3
  986.4 23.7 %copy-start.24 = (f32[1152]{0:T(1024)S(1)}, f32[1152]{0:T(1024)}, u32[]{:S(2)}) copy-start(f32[1152]{0:T(1024)} %get-tuple-element.6) | copy-start | bytes 13828
  988.0 62.1 %reduce-scatter.29.cloned.1.call-start = ((), (), s32[]{:S(2)}) async-start(), calls=%async_computation.24 | async-start | bytes 884736 | tf_op jit(solution)/shard_map/reduce_scatter | solution.py:137
  (35 other events, 227.2 us)
Sparse Core Ops, SparseCore 0:
  10.5 76.1 all-gather.16
  89.7 89.5 all-gather.14
  182.3 123.2 all-gather.12
  352.7 18.1 reduce-scatter.10
  374.2 118.5 all-gather.20
  496.2 115.8 all-gather.18
  627.8 16.1 reduce-scatter.12
  685.0 19.3 reduce-scatter.14
  728.1 19.6 reduce-scatter.16
  786.7 19.5 reduce-scatter.18
  829.8 19.5 reduce-scatter.20
  888.2 19.7 reduce-scatter.22
  931.6 19.5 reduce-scatter.24
  988.1 19.6 reduce-scatter.26
  1030.4 19.6 reduce-scatter.28
